TPU v7x, 32 devices: a whole 2x2x4 slice. The times are simulated.
32 devices in a mesh: gx: 4 (over z), gy: 8 (over y, x, core).
Axes of the slice: x: 2, y: 2, z: 4, core: 2. Of those that a mesh axis runs over, the one named last changes fastest.
Arguments:
- adjoint_rhs: float32 [2, 3, 4, 512, 128], P(None, None, 'gx', 'gy'), may hold values from -6 to 6
- block_inverse: float32 [3, 3, 4, 512, 128], P(None, None, 'gx', 'gy'), may hold values from -0.3 to 1.3, as said below
- x_couplings: float32 [2, 3, 4, 512, 128], P(None, None, 'gx', 'gy'), may hold values from -0.8 to -0.3
- y_couplings: float32 [2, 3, 4, 512, 128], P(None, None, 'gx', 'gy'), may hold values from -0.3 to -0.05
- perf_cell: int32 [2048], P(('gx', 'gy')), may hold values from 0 to 8191
- perf_well: int32 [2048], P(('gx', 'gy')), may hold values from 0 to 127
- perf_weight: float32 [2048], P(('gx', 'gy')), may hold values from 0.5 to 2
- well_adjoint: float32 [3, 128], P(None, ('gx', 'gy')), may hold values from -6 to 6
Outputs:
- precond: float32 [2, 3, 4, 512, 128], P(None, None, 'gx', 'gy')
- well_update: float32 [3, 128], P(None, ('gx', 'gy'))
Inputs may be any that keep to these rules, and one draw needn't show every extreme that they name: `perf_cell`: local cell index within the owning device's block. `block_inverse`: diagonal entries are at least 0.5, off-diagonal ones at most 0.3 in magnitude.
All inputs are finite; a program needn't handle non-finite values.
Results may differ from a plain program's by a relative error of at most 0.00017.
Values sent between devices are 32-bit elements; how exact they have to be, the bound alone decides.
A program may use at most 64 MiB of HBM per device.

v0:
```python
import jax
import jax.numpy as jnp
from jax import lax
from jax.sharding import PartitionSpec as P


def passed_along(block, axis, distance):
    devices = range(lax.axis_size(axis))
    route = [(i - distance, i) for i in devices if i - distance in devices]
    return lax.ppermute(block, axis, route)


def with_halo(shard, sides, width):
    for axis, dim in sides:
        peers, length = (lax.axis_size(axis), shard.shape[dim])
        up = [(i, (i + 1) % peers) for i in range(peers - 1)]
        down = [(j, i) for i, j in up]
        last = lax.slice_in_dim(shard, length - width, length, axis=dim)
        first = lax.slice_in_dim(shard, 0, width, axis=dim)
        before = lax.ppermute(last, axis, up)
        after = lax.ppermute(first, axis, down)
        shard = jnp.concatenate([before, shard, after], axis=dim)
    return shard


def apply_inverse(inverse, values):
    return (
        inverse[:, 0] * values[None, 0]
        + inverse[:, 1] * values[None, 1]
        + inverse[:, 2] * values[None, 2]
    )


def couple(values, padded, inverse, lower, upper):
    return apply_inverse(inverse, values - lower * padded[:, :, :-2] - upper * padded[:, :, 2:])


def pad_lines(weighted):
    return jnp.pad(weighted, ((0, 0), (0, 0), (1, 1), (0, 0)))


def plane_solve(values, inverse, lower, upper):
    weighted = apply_inverse(inverse, values)
    padded = pad_lines(weighted)
    return couple(values, padded, inverse, lower, upper)


def march_forward(sources, block_inverse, x_low, lower, upper, inflow):
    planes = sources.shape[2]

    def step(plane, state):
        result, previous = state
        inverse = lax.dynamic_index_in_dim(block_inverse, plane, 2, True)
        low = lax.dynamic_index_in_dim(x_low, plane, 1, True)
        ylo = lax.dynamic_index_in_dim(lower, plane, 1, True)
        yup = lax.dynamic_index_in_dim(upper, plane, 1, True)
        source = lax.dynamic_index_in_dim(sources, plane, 2, False)
        current = plane_solve(source - low * previous, inverse, ylo, yup)
        result = lax.dynamic_update_index_in_dim(result, current, plane, 2)
        return (result, current)

    result, _ = lax.fori_loop(0, planes, step, (jnp.zeros_like(sources), inflow))
    return result


def march_backward(forward_planes, block_inverse, x_up, lower, upper, outflow):
    planes = forward_planes.shape[2]

    def step(count, state):
        result, following = state
        plane = planes - 1 - count
        inverse = lax.dynamic_index_in_dim(block_inverse, plane, 2, True)
        high = lax.dynamic_index_in_dim(x_up, plane, 1, True)
        ylo = lax.dynamic_index_in_dim(lower, plane, 1, True)
        yup = lax.dynamic_index_in_dim(upper, plane, 1, True)
        current_q = lax.dynamic_index_in_dim(forward_planes, plane, 2, False)
        current = current_q - plane_solve(high * following, inverse, ylo, yup)
        result = lax.dynamic_update_index_in_dim(result, current, plane, 2)
        return (result, current)

    result, _ = lax.fori_loop(0, planes, step, (jnp.zeros_like(forward_planes), outflow))
    return result


def precondition(rhs_cells, block_inverse, x_couplings, y_couplings):
    chain_size = lax.axis_size("gx")
    lower = y_couplings[0]
    upper = y_couplings[1]
    boundary_shape = (
        rhs_cells.shape[0],
        rhs_cells.shape[1],
        rhs_cells.shape[3],
        rhs_cells.shape[4],
    )
    inflow = jnp.zeros(boundary_shape, jnp.float32)
    forward_planes = rhs_cells
    for turn in range(chain_size):
        forward_planes = march_forward(
            rhs_cells, block_inverse, x_couplings[0], lower, upper, inflow
        )
        if turn + 1 < chain_size:
            inflow = passed_along(forward_planes[:, :, -1], "gx", 1)
    outflow = jnp.zeros(boundary_shape, jnp.float32)
    result = forward_planes
    for turn in range(chain_size):
        result = march_backward(
            forward_planes, block_inverse, x_couplings[1], lower, upper, outflow
        )
        if turn + 1 < chain_size:
            outflow = passed_along(result[:, :, 0], "gx", -1)
    return result


def both_applications(rhs_cells, block_inverse, x_couplings, y_couplings):
    first = precondition(rhs_cells[:, 0:1], block_inverse, x_couplings, y_couplings)
    second = precondition(rhs_cells[:, 1:2], block_inverse, x_couplings, y_couplings)
    return jnp.concatenate([first, second], axis=1)


def per_device(
    adjoint_rhs,
    block_inverse,
    x_couplings,
    y_couplings,
    perf_cell,
    perf_well,
    perf_weight,
    well_adjoint,
):
    all_wells = lax.all_gather(well_adjoint, ("gx", "gy"), axis=1, tiled=True)
    well_count = all_wells.shape[1]
    selector = (perf_well[:, None] == jnp.arange(well_count, dtype=jnp.int32)[None, :]).astype(
        jnp.float32
    )
    picked = jnp.dot(all_wells, selector.T, precision=lax.Precision.HIGHEST)
    terms = picked * perf_weight[None]
    comps = adjoint_rhs.shape[1]
    block_shape = adjoint_rhs.shape[2:]
    planes = block_shape[0]
    lines = block_shape[1]
    depth_cells = block_shape[2]
    cells = planes * lines * depth_cells
    source = jnp.zeros((comps, cells), jnp.float32).at[:, perf_cell].add(terms)
    source = source.reshape((comps,) + block_shape)
    rhs_cells = jnp.moveaxis(adjoint_rhs + source[None], 0, 1)
    margin_lines = 2 * planes * lax.axis_size("gx") + 1
    stacked = jnp.concatenate(
        [
            rhs_cells.reshape(comps * 2, planes, lines, depth_cells),
            block_inverse.reshape(comps * comps, planes, lines, depth_cells),
            x_couplings.reshape(2 * comps, planes, lines, depth_cells),
            y_couplings.reshape(2 * comps, planes, lines, depth_cells),
        ],
        axis=0,
    )
    extended = with_halo(stacked, (("gy", 2),), margin_lines)
    wide_lines = extended.shape[2]
    first_end = comps * 2
    second_end = first_end + comps * comps
    third_end = second_end + 2 * comps
    wide_rhs = extended[:first_end].reshape(comps, 2, planes, wide_lines, depth_cells)
    wide_inverse = extended[first_end:second_end].reshape(
        comps, comps, planes, wide_lines, depth_cells
    )
    wide_x = extended[second_end:third_end].reshape(2, comps, planes, wide_lines, depth_cells)
    wide_y = extended[third_end:].reshape(2, comps, planes, wide_lines, depth_cells)
    wide_solved = both_applications(wide_rhs, wide_inverse, wide_x, wide_y)
    solved = wide_solved[:, :, :, margin_lines : margin_lines + lines]
    precond = jnp.moveaxis(solved, 1, 0)
    second_flat = precond[1].reshape(comps, cells)
    values = jnp.take(second_flat, perf_cell, axis=1) * perf_weight[None]
    local_sums = jnp.dot(values, selector, precision=lax.Precision.HIGHEST)
    well_update = lax.psum_scatter(local_sums, ("gx", "gy"), scatter_dimension=1, tiled=True)
    return (precond, well_update)


def solution(mesh):
    placed = (
        P(None, None, "gx", "gy", None),
        P(None, None, "gx", "gy", None),
        P(None, None, "gx", "gy", None),
        P(None, None, "gx", "gy", None),
        P(("gx", "gy")),
        P(("gx", "gy")),
        P(("gx", "gy")),
        P(None, ("gx", "gy")),
    )
    return jax.shard_map(
        per_device,
        mesh=mesh,
        in_specs=placed,
        out_specs=(P(None, None, "gx", "gy", None), P(None, ("gx", "gy"))),
        check_vma=False,
    )
```

profile of v0, /device:TPU:0, one launch (start us, length us, event | category | flops | bytes accessed | tf_op | source)
XLA Modules:
  0.0 183.9 jit_solution(16767146702352466748)
XLA Ops:
  0.6 0.7 compare_select_fusion
  1.3 0.8 copy.30
  2.1 43.4 %all-gather = f32[32,4,3]{2,1,0:T(4,128)S(1)} all-gather(f32[1,4,3]{2,1,0:T(4,128)S(1)} %bitcast.879), channel_id=1, replica_groups=mesh['gx'=4,'gy'=8] {'gx','gy'}, dimensions={0}, use_global_device_ids=true | all-gather | bytes 1584 | tf_op jit(solution)/shard_map/all_gather | solution.py:130
  45.5 0.9 convolution_multiply_fusion
  46.4 3.0 %scatter_custom_fusion = f32[3,8192]{0,1:T(8,128)} fusion(s32[64]{0:T(128)S(1)} %compare_select_fusion, f32[64,3]{1,0:T(8,128)S(1)} %copy.31, f32[]{:T(128)} %constant.310.clone.1), kind=kCustom, calls=%fused_computation.2 | custom fusion | flops 192 | bytes 98308 | tf_op jit(solution)/shard_map/scatter-add | solution.py:143
  49.5 2.9 %copy.32 = f32[3,64,128]{2,1,0:T(8,128)S(1)} copy(f32[3,64,128]{0,2,1:T(8,128)} %bitcast.749) | data formatting | bytes 196608 | tf_op jit(solution)/shard_map/add | solution.py:145
  52.5 0.3 pad_maximum_fusion.9
  52.8 2.3 %collective-permute-start = (f32[27,1,9,128]{3,1,2,0:T(1,128)S(1)}, f32[27,1,9,128]{3,1,2,0:T(1,128)S(1)}, u32[]{:S(2)}, u32[]{:S(2)}) collective-permute-start(f32[27,1,9,128]{3,1,2,0:T(1,128)S(1)} %get-tuple-element.312), channel_id=1, source_target_pairs={{0,1},{1,2},{2,3},{3,4},{4,5},{5,6},{6,7},{8,9},{9,10},{10,11},{11... | collective-permute-start | bytes 373256 | tf_op jit(solution)/shard_map/ppermute | solution.py:20
  55.0 1.3 collective-permute-start.1
  56.4 1.9 %collective-permute-done.1 = f32[27,1,9,128]{3,1,2,0:T(1,128)S(1)} collective-permute-done((f32[27,1,9,128]{3,1,2,0:T(1,128)S(1)}, f32[27,1,9,128]{3,1,2,0:T(1,128)S(1)}, u32[]{:S(2)}, u32[]{:S(2)}) %collective-permute-start.1) | collective-permute-done | bytes 124448 | tf_op jit(solution)/shard_map/ppermute | solution.py:21
  58.3 6.0 %pad_maximum_fusion = f32[27,1,82,128]{3,1,2,0:T(1,128)S(1)} fusion(f32[27,1,9,128]{3,1,2,0:T(1,128)S(1)} %collective-permute-done.1, f32[6,1,64,128]{3,1,2,0:T(1,128)S(1)} %bitcast.765, f32[6,1,64,128]{3,1,2,0:T(1,128)S(1)} %bitcast.769, f32[9,1,64,128]{3,1,2,0:T(1,128)S(1)} %bitcast.760, f32[6,1,64,128]{3,1,2,0:T(1,128)S(1)} %bitcast.756, ...), kind=kLoop, calls=%fused_computation.4 | loop fusion | flops 1416960 | bytes 2267136 | tf_op jit(solution)/shard_map/concatenate | solution.py:22
  64.3 0.4 broadcast_multiply_fusion
  65.0 0.3 fusion.20
  65.4 0.4 multiply_subtract_fusion.20
  66.1 0.4 fusion.4
  66.5 1.3 collective-permute-start.2
  67.8 1.3 collective-permute-start.8
  69.1 1.1 collective-permute-done.2
  70.3 1.7 collective-permute-done.8
  72.0 0.3 multiply_subtract_fusion.19
  72.4 0.4 fusion.5
  72.8 0.4 multiply_subtract_fusion.18
  73.2 0.4 fusion.6
  73.6 4.4 %collective-permute-start.3 = (f32[3,1,82,128]{3,1,2,0:T(1,128)S(1)}, f32[3,1,82,128]{3,1,2,0:T(1,128)S(1)}, u32[]{:S(2)}, u32[]{:S(2)}) collective-permute-start(f32[3,1,82,128]{3,1,2,0:T(1,128)S(1)} %get-tuple-element.362), channel_id=1, source_target_pairs={{0,8},{8,16},{16,24},{1,9},{9,17},{17,25},{2,10},{10,18},{18,26},{... | collective-permute-start | bytes 377864 | tf_op jit(solution)/shard_map/ppermute | solution.py:10
  78.0 1.9 %collective-permute-start.9 = (f32[3,1,82,128]{3,1,2,0:T(1,128)S(1)}, f32[3,1,82,128]{3,1,2,0:T(1,128)S(1)}, u32[]{:S(2)}, u32[]{:S(2)}) collective-permute-start(f32[3,1,82,128]{3,1,2,0:T(1,128)S(1)} %get-tuple-element.363), channel_id=1, source_target_pairs={{0,8},{8,16},{16,24},{1,9},{9,17},{17,25},{2,10},{10,18},{18,26},{... | collective-permute-start | bytes 377864 | tf_op jit(solution)/shard_map/ppermute | solution.py:10
  79.9 0.7 collective-permute-done.3
  80.6 3.1 %collective-permute-done.9 = f32[3,1,82,128]{3,1,2,0:T(1,128)S(1)} collective-permute-done((f32[3,1,82,128]{3,1,2,0:T(1,128)S(1)}, f32[3,1,82,128]{3,1,2,0:T(1,128)S(1)}, u32[]{:S(2)}, u32[]{:S(2)}) %collective-permute-start.9) | collective-permute-done | bytes 125984 | tf_op jit(solution)/shard_map/ppermute | solution.py:10
  83.7 0.3 multiply_subtract_fusion.17
  84.1 0.4 fusion.7
  84.5 0.4 multiply_subtract_fusion.16
  85.0 0.4 fusion.8
  85.4 4.4 %collective-permute-start.10 = (f32[3,1,82,128]{3,1,2,0:T(1,128)S(1)}, f32[3,1,82,128]{3,1,2,0:T(1,128)S(1)}, u32[]{:S(2)}, u32[]{:S(2)}) collective-permute-start(f32[3,1,82,128]{3,1,2,0:T(1,128)S(1)} %get-tuple-element.348), channel_id=1, source_target_pairs={{0,8},{8,16},{16,24},{1,9},{9,17},{17,25},{2,10},{10,18},{18,26},{... | collective-permute-start | bytes 377864 | tf_op jit(solution)/shard_map/ppermute | solution.py:10
  89.8 2.1 %collective-permute-start.4 = (f32[3,1,82,128]{3,1,2,0:T(1,128)S(1)}, f32[3,1,82,128]{3,1,2,0:T(1,128)S(1)}, u32[]{:S(2)}, u32[]{:S(2)}) collective-permute-start(f32[3,1,82,128]{3,1,2,0:T(1,128)S(1)} %get-tuple-element.347), channel_id=1, source_target_pairs={{0,8},{8,16},{16,24},{1,9},{9,17},{17,25},{2,10},{10,18},{18,26},{... | collective-permute-start | bytes 377864 | tf_op jit(solution)/shard_map/ppermute | solution.py:10
  91.9 1.6 collective-permute-done.10
  93.5 2.3 %collective-permute-done.4 = f32[3,1,82,128]{3,1,2,0:T(1,128)S(1)} collective-permute-done((f32[3,1,82,128]{3,1,2,0:T(1,128)S(1)}, f32[3,1,82,128]{3,1,2,0:T(1,128)S(1)}, u32[]{:S(2)}, u32[]{:S(2)}) %collective-permute-start.4) | collective-permute-done | bytes 125984 | tf_op jit(solution)/shard_map/ppermute | solution.py:10
  95.8 0.3 multiply_subtract_fusion.15
  96.3 0.5 fusion.9
  96.8 0.5 multiply_subtract_fusion.14
  97.5 0.6 fusion.83
  98.1 1.3 collective-permute-start.5
  99.4 1.3 collective-permute-start.11
  100.7 5.8 %collective-permute-done.5 = f32[3,1,82,128]{3,1,2,0:T(1,128)S(1)} collective-permute-done((f32[3,1,82,128]{3,1,2,0:T(1,128)S(1)}, f32[3,1,82,128]{3,1,2,0:T(1,128)S(1)}, u32[]{:S(2)}, u32[]{:S(2)}) %collective-permute-start.5) | collective-permute-done | bytes 125984 | tf_op jit(solution)/shard_map/ppermute | solution.py:10
  107.2 0.4 fusion.15
  107.6 1.3 collective-permute-start.6
  108.9 5.5 %collective-permute-done.6 = f32[3,1,82,128]{3,1,2,0:T(1,128)S(1)} collective-permute-done((f32[3,1,82,128]{3,1,2,0:T(1,128)S(1)}, f32[3,1,82,128]{3,1,2,0:T(1,128)S(1)}, u32[]{:S(2)}, u32[]{:S(2)}) %collective-permute-start.6) | collective-permute-done | bytes 125984 | tf_op jit(solution)/shard_map/ppermute | solution.py:10
  114.7 0.3 fusion.16
  115.1 0.4 multiply_subtract_fusion.11
  115.6 0.7 fusion.18
  116.3 1.3 collective-permute-start.12
  117.6 1.3 collective-permute-start.7
  119.0 4.2 %collective-permute-done.12 = f32[3,1,82,128]{3,1,2,0:T(1,128)S(1)} collective-permute-done((f32[3,1,82,128]{3,1,2,0:T(1,128)S(1)}, f32[3,1,82,128]{3,1,2,0:T(1,128)S(1)}, u32[]{:S(2)}, u32[]{:S(2)}) %collective-permute-start.12) | collective-permute-done | bytes 125984 | tf_op jit(solution)/shard_map/ppermute | solution.py:10
  123.1 1.9 %collective-permute-done.7 = f32[3,1,82,128]{3,1,2,0:T(1,128)S(1)} collective-permute-done((f32[3,1,82,128]{3,1,2,0:T(1,128)S(1)}, f32[3,1,82,128]{3,1,2,0:T(1,128)S(1)}, u32[]{:S(2)}, u32[]{:S(2)}) %collective-permute-start.7) | collective-permute-done | bytes 125984 | tf_op jit(solution)/shard_map/ppermute | solution.py:10
  125.4 0.3 fusion.19
  125.7 0.4 multiply_subtract_fusion.10
  126.1 0.4 fusion.33
  126.5 1.3 collective-permute-start.13
  127.9 5.4 %collective-permute-done.13 = f32[3,1,82,128]{3,1,2,0:T(1,128)S(1)} collective-permute-done((f32[3,1,82,128]{3,1,2,0:T(1,128)S(1)}, f32[3,1,82,128]{3,1,2,0:T(1,128)S(1)}, u32[]{:S(2)}, u32[]{:S(2)}) %collective-permute-start.13) | collective-permute-done | bytes 125984 | tf_op jit(solution)/shard_map/ppermute | solution.py:10
  133.5 0.3 fusion.34
  134.1 0.7 fusion.38
  135.1 0.7 copy.40
  135.8 2.7 %copy.38 = f32[1,3,1,64,128]{1,4,3,2,0:T(8,128)} copy(f32[1,3,1,64,128]{4,0,3,2,1:T(1,128)S(1)} %slice.942) | data formatting | bytes 196608 | tf_op jit(solution)/shard_map/slice | solution.py:170
  138.5 2.8 %gather_fusion = f32[64,3]{1,0:T(8,128)S(1)} fusion(f32[3,8192]{0,1:T(8,128)} %bitcast.763, s32[1024]{0:T(1024)S(1)} %pad_clamp_fusion), kind=kCustom, calls=%fused_computation | custom fusion | bytes 1792 | tf_op jit(solution)/shard_map/jit(_take)/gather | solution.py:171
  141.5 41.7 %all-reduce.15 = f32[3,128]{1,0:T(4,128)S(1)} all-reduce(f32[3,128]{1,0:T(4,128)S(1)} %fusion.73), channel_id=2, replica_groups=mesh['gx'=4,'gy'=8] {'gx','gy'}, use_global_device_ids=true, to_apply=%region_1.2.clone | all-reduce | flops 384 | bytes 3072
  183.3 0.6 constant_dynamic-slice_fusion
  (154 shorter events, 3.4 us)
Async XLA Ops:
  49.5 2.9 %copy-start.3 = (f32[2,3,1,64,128]{4,3,2,1,0:T(8,128)S(1)}, f32[2,3,1,64,128]{4,3,2,1,0:T(8,128)}, u32[]{:S(2)}) copy-start(f32[2,3,1,64,128]{4,3,2,1,0:T(8,128)} %param.8) | copy-start | bytes 589828
  49.5 3.0 %copy-start = (f32[3,3,1,64,128]{4,3,2,1,0:T(8,128)S(1)}, f32[3,3,1,64,128]{4,3,2,1,0:T(8,128)}, u32[]{:S(2)}) copy-start(f32[3,3,1,64,128]{4,3,2,1,0:T(8,128)} %param.9) | copy-start | bytes 884740
  49.5 3.0 %copy-start.1 = (f32[2,3,1,64,128]{4,3,2,1,0:T(8,128)S(1)}, f32[2,3,1,64,128]{4,3,2,1,0:T(8,128)}, u32[]{:S(2)}) copy-start(f32[2,3,1,64,128]{4,3,2,1,0:T(8,128)} %param.11) | copy-start | bytes 589828
  49.5 3.0 %copy-start.2 = (f32[2,3,1,64,128]{4,3,2,1,0:T(8,128)S(1)}, f32[2,3,1,64,128]{4,3,2,1,0:T(8,128)}, u32[]{:S(2)}) copy-start(f32[2,3,1,64,128]{4,3,2,1,0:T(8,128)} %param.10) | copy-start | bytes 589828
  52.8 3.6 %collective-permute-start = (f32[27,1,9,128]{3,1,2,0:T(1,128)S(1)}, f32[27,1,9,128]{3,1,2,0:T(1,128)S(1)}, u32[]{:S(2)}, u32[]{:S(2)}) collective-permute-start(f32[27,1,9,128]{3,1,2,0:T(1,128)S(1)} %get-tuple-element.312), channel_id=1, source_target_pairs={{0,1},{1,2},{2,3},{3,4},{4,5},{5,6},{6,7},{8,9},{9,10},{10,11},{11... | collective-permute-start | bytes 373256 | tf_op jit(solution)/shard_map/ppermute | solution.py:20
  55.0 3.2 %collective-permute-start.1 = (f32[27,1,9,128]{3,1,2,0:T(1,128)S(1)}, f32[27,1,9,128]{3,1,2,0:T(1,128)S(1)}, u32[]{:S(2)}, u32[]{:S(2)}) collective-permute-start(f32[27,1,9,128]{3,1,2,0:T(1,128)S(1)} %get-tuple-element.313), channel_id=1, source_target_pairs={{1,0},{2,1},{3,2},{4,3},{5,4},{6,5},{7,6},{9,8},{10,9},{11,10},{12... | collective-permute-start | bytes 373256 | tf_op jit(solution)/shard_map/ppermute | solution.py:21
  66.5 3.8 %collective-permute-start.2 = (f32[3,1,82,128]{3,1,2,0:T(1,128)S(1)}, f32[3,1,82,128]{3,1,2,0:T(1,128)S(1)}, u32[]{:S(2)}, u32[]{:S(2)}) collective-permute-start(f32[3,1,82,128]{3,1,2,0:T(1,128)S(1)} %get-tuple-element.368), channel_id=1, source_target_pairs={{0,8},{8,16},{16,24},{1,9},{9,17},{17,25},{2,10},{10,18},{18,26},{... | collective-permute-start | bytes 377864 | tf_op jit(solution)/shard_map/ppermute | solution.py:10
  67.8 4.2 %collective-permute-start.8 = (f32[3,1,82,128]{3,1,2,0:T(1,128)S(1)}, f32[3,1,82,128]{3,1,2,0:T(1,128)S(1)}, u32[]{:S(2)}, u32[]{:S(2)}) collective-permute-start(f32[3,1,82,128]{3,1,2,0:T(1,128)S(1)} %get-tuple-element.378), channel_id=1, source_target_pairs={{0,8},{8,16},{16,24},{1,9},{9,17},{17,25},{2,10},{10,18},{18,26},{... | collective-permute-start | bytes 377864 | tf_op jit(solution)/shard_map/ppermute | solution.py:10
  73.6 7.0 %collective-permute-start.3 = (f32[3,1,82,128]{3,1,2,0:T(1,128)S(1)}, f32[3,1,82,128]{3,1,2,0:T(1,128)S(1)}, u32[]{:S(2)}, u32[]{:S(2)}) collective-permute-start(f32[3,1,82,128]{3,1,2,0:T(1,128)S(1)} %get-tuple-element.362), channel_id=1, source_target_pairs={{0,8},{8,16},{16,24},{1,9},{9,17},{17,25},{2,10},{10,18},{18,26},{... | collective-permute-start | bytes 377864 | tf_op jit(solution)/shard_map/ppermute | solution.py:10
  78.0 5.7 %collective-permute-start.9 = (f32[3,1,82,128]{3,1,2,0:T(1,128)S(1)}, f32[3,1,82,128]{3,1,2,0:T(1,128)S(1)}, u32[]{:S(2)}, u32[]{:S(2)}) collective-permute-start(f32[3,1,82,128]{3,1,2,0:T(1,128)S(1)} %get-tuple-element.363), channel_id=1, source_target_pairs={{0,8},{8,16},{16,24},{1,9},{9,17},{17,25},{2,10},{10,18},{18,26},{... | collective-permute-start | bytes 377864 | tf_op jit(solution)/shard_map/ppermute | solution.py:10
  85.4 8.2 %collective-permute-start.10 = (f32[3,1,82,128]{3,1,2,0:T(1,128)S(1)}, f32[3,1,82,128]{3,1,2,0:T(1,128)S(1)}, u32[]{:S(2)}, u32[]{:S(2)}) collective-permute-start(f32[3,1,82,128]{3,1,2,0:T(1,128)S(1)} %get-tuple-element.348), channel_id=1, source_target_pairs={{0,8},{8,16},{16,24},{1,9},{9,17},{17,25},{2,10},{10,18},{18,26},{... | collective-permute-start | bytes 377864 | tf_op jit(solution)/shard_map/ppermute | solution.py:10
  89.8 6.1 %collective-permute-start.4 = (f32[3,1,82,128]{3,1,2,0:T(1,128)S(1)}, f32[3,1,82,128]{3,1,2,0:T(1,128)S(1)}, u32[]{:S(2)}, u32[]{:S(2)}) collective-permute-start(f32[3,1,82,128]{3,1,2,0:T(1,128)S(1)} %get-tuple-element.347), channel_id=1, source_target_pairs={{0,8},{8,16},{16,24},{1,9},{9,17},{17,25},{2,10},{10,18},{18,26},{... | collective-permute-start | bytes 377864 | tf_op jit(solution)/shard_map/ppermute | solution.py:10
  98.1 8.4 %collective-permute-start.5 = (f32[3,1,82,128]{3,1,2,0:T(1,128)S(1)}, f32[3,1,82,128]{3,1,2,0:T(1,128)S(1)}, u32[]{:S(2)}, u32[]{:S(2)}) collective-permute-start(f32[3,1,82,128]{3,1,2,0:T(1,128)S(1)} %get-tuple-element.314), channel_id=1, source_target_pairs={{8,0},{16,8},{24,16},{9,1},{17,9},{25,17},{10,2},{18,10},{26,18},{... | collective-permute-start | bytes 377864 | tf_op jit(solution)/shard_map/ppermute | solution.py:10
  99.4 9.5 %collective-permute-start.11 = (f32[3,1,82,128]{3,1,2,0:T(1,128)S(1)}, f32[3,1,82,128]{3,1,2,0:T(1,128)S(1)}, u32[]{:S(2)}, u32[]{:S(2)}) collective-permute-start(f32[3,1,82,128]{3,1,2,0:T(1,128)S(1)} %get-tuple-element.324), channel_id=1, source_target_pairs={{8,0},{16,8},{24,16},{9,1},{17,9},{25,17},{10,2},{18,10},{26,18},{... | collective-permute-start | bytes 377864 | tf_op jit(solution)/shard_map/ppermute | solution.py:10
  107.6 6.8 %collective-permute-start.6 = (f32[3,1,82,128]{3,1,2,0:T(1,128)S(1)}, f32[3,1,82,128]{3,1,2,0:T(1,128)S(1)}, u32[]{:S(2)}, u32[]{:S(2)}) collective-permute-start(f32[3,1,82,128]{3,1,2,0:T(1,128)S(1)} %fusion.15), channel_id=1, source_target_pairs={{8,0},{16,8},{24,16},{9,1},{17,9},{25,17},{10,2},{18,10},{26,18},{... | collective-permute-start | bytes 377864 | tf_op jit(solution)/shard_map/ppermute | solution.py:10
  115.4 3.5 %copy-start.6 = (s32[64]{0:T(128)S(1)}, s32[64]{0:T(128)}, u32[]{:S(2)}) copy-start(s32[64]{0:T(128)} %param.12) | copy-start | bytes 772
  116.3 6.8 %collective-permute-start.12 = (f32[3,1,82,128]{3,1,2,0:T(1,128)S(1)}, f32[3,1,82,128]{3,1,2,0:T(1,128)S(1)}, u32[]{:S(2)}, u32[]{:S(2)}) collective-permute-start(f32[3,1,82,128]{3,1,2,0:T(1,128)S(1)} %get-tuple-element.330), channel_id=1, source_target_pairs={{8,0},{16,8},{24,16},{9,1},{17,9},{25,17},{10,2},{18,10},{26,18},{... | collective-permute-start | bytes 377864 | tf_op jit(solution)/shard_map/ppermute | solution.py:10
  117.6 7.4 %collective-permute-start.7 = (f32[3,1,82,128]{3,1,2,0:T(1,128)S(1)}, f32[3,1,82,128]{3,1,2,0:T(1,128)S(1)}, u32[]{:S(2)}, u32[]{:S(2)}) collective-permute-start(f32[3,1,82,128]{3,1,2,0:T(1,128)S(1)} %get-tuple-element.329), channel_id=1, source_target_pairs={{8,0},{16,8},{24,16},{9,1},{17,9},{25,17},{10,2},{18,10},{26,18},{... | collective-permute-start | bytes 377864 | tf_op jit(solution)/shard_map/ppermute | solution.py:10
  126.5 6.8 %collective-permute-start.13 = (f32[3,1,82,128]{3,1,2,0:T(1,128)S(1)}, f32[3,1,82,128]{3,1,2,0:T(1,128)S(1)}, u32[]{:S(2)}, u32[]{:S(2)}) collective-permute-start(f32[3,1,82,128]{3,1,2,0:T(1,128)S(1)} %fusion.33), channel_id=1, source_target_pairs={{8,0},{16,8},{24,16},{9,1},{17,9},{25,17},{10,2},{18,10},{26,18},{... | collective-permute-start | bytes 377864 | tf_op jit(solution)/shard_map/ppermute | solution.py:10
  135.8 5.5 %copy-start.4 = (s32[64]{0:T(128)S(1)}, s32[64]{0:T(128)}, u32[]{:S(2)}) copy-start(s32[64]{0:T(128)} %param.13) | copy-start | bytes 772
  135.8 5.5 %copy-start.5 = (f32[64]{0:T(128)S(1)}, f32[64]{0:T(128)}, u32[]{:S(2)}) copy-start(f32[64]{0:T(128)} %param.14) | copy-start | bytes 772
where the time goes:
time: 185 us; the launch traced here: 184 us
  blocking collectives  85.1 us (46%)
  waiting for transfers between devices  35.3 us (19%)
  starting transfers between devices  26.7 us (14%)
  other arithmetic  22 us (12%)
  local copies, waits for them, and re-layouts  11.7 us (6%)
  between operations  2 us (1%)
    all_gather x1, blocking collectives, per_device(): all_wells = lax.all_gather(well_adjoint, ('gx', 'gy'), axis=1, tiled=True)  43.4 us
    unnamed x1, blocking collectives  41.7 us
    ppermute x12, waiting for transfers between devices, passed_along(): return lax.ppermute(block, axis, route)  33.4 us
    ppermute x12, starting transfers between devices, passed_along(): return lax.ppermute(block, axis, route)  23.2 us
    concatenate x1, other arithmetic, with_halo(): shard = jnp.concatenate([before, shard, after], axis=dim)  5.97 us
    add x11, other arithmetic, apply_inverse(): inverse[:, 0] * values[None, 0] + inverse[:, 1] * values[None, 1]  3.86 us
  transfers between devices with their start and end apart: 14, of which 12 were waited for; matrix products, arithmetic and copies ran while one was open for 1% of the time, Pallas kernels for 0%

commit v1 on v0

v1 whole, which is shorter than its diff:
```python
import functools

import jax
import jax.numpy as jnp
from jax import lax
from jax.experimental import pallas as pl
from jax.experimental.pallas import tpu as pltpu
from jax.sharding import PartitionSpec as P

MESH = pl.DeviceIdType.MESH
SUB = 8
LANES = 128
HIGHEST = lax.Precision.HIGHEST


def round_up(value, step):
    return -(-value // step) * step


def apply_inverse(inverse, values):
    comps = range(len(values))
    rows = []
    for c in comps:
        total = inverse[c][0] * values[0]
        for d in comps[1:]:
            total = total + inverse[c][d] * values[d]
        rows.append(total)
    return rows


def kernel(
    dims,
    rhs_h,
    inv_h,
    xc_h,
    yc_h,
    cell_ref,
    well_ref,
    weight_ref,
    adjoint_ref,
    out_ref,
    update_ref,
    rhs_s,
    inv_s,
    xc_s,
    yc_s,
    src_s,
    fwd_in,
    bwd_in,
    q_s,
    p_s,
    v_s,
    w_s,
    perf_s,
    ag1,
    ag2,
    rs1,
    rs2,
    load_sem,
    halo_send,
    halo_recv,
    ag1_send,
    ag1_recv,
    ag2_send,
    ag2_recv,
    rs1_send,
    rs1_recv,
    rs2_send,
    rs2_recv,
    fwd_send,
    fwd_recv,
    bwd_send,
    bwd_recv,
):
    n_gx, n_gy, ks, comps, inner, margin, depth, perfs, own_wells = dims
    groups = inner + 2 * margin
    a = lax.axis_index("gx")
    b = lax.axis_index("gy")

    loads = [
        pltpu.make_async_copy(src, dst.at[:, :, pl.ds(margin, inner)], load_sem.at[n])
        for n, (src, dst) in enumerate(
            ((rhs_h, rhs_s), (inv_h, inv_s), (xc_h, xc_s), (yc_h, yc_s))
        )
    ]
    for copy in loads:
        copy.start()

    barrier = pltpu.get_barrier_semaphore()
    for d in range(1, n_gy):
        pl.semaphore_signal(
            barrier, inc=1, device_id=(a, lax.rem(b + d, n_gy)), device_id_type=MESH
        )
    for d in range(1, n_gx):
        pl.semaphore_signal(
            barrier, inc=1, device_id=(lax.rem(a + d, n_gx), b), device_id_type=MESH
        )

    lane = lax.broadcasted_iota(jnp.int32, (comps, ag1.shape[2]), 1)
    first_well = (a * n_gy + b) * own_wells
    tile = jnp.zeros((comps, ag1.shape[2]), jnp.float32)
    for w in range(own_wells):
        tile = jnp.where(lane == first_well + w, adjoint_ref[:, w : w + 1], tile)
    ag1[0] = jnp.zeros(ag1.shape[1:], jnp.float32)
    ag1[0, 0:comps] = tile
    perf_s[0] = jnp.zeros(perf_s.shape[1:], jnp.float32)
    perf_s[0, 0:1, 0:perfs] = cell_ref[...].astype(jnp.float32)
    perf_s[0, 1:2, 0:perfs] = well_ref[...].astype(jnp.float32)
    perf_s[0, 2:3, 0:perfs] = weight_ref[...]

    zero_edges = ((0, b == 0, 0), (1, b == n_gy - 1, margin + inner))
    for side, missing, start in zero_edges:

        @pl.when(missing)
        def _():
            perf_s[1 + side] = jnp.zeros(perf_s.shape[1:], jnp.float32)
            for ref in (rhs_s, inv_s, xc_s, yc_s):
                ref[:, :, start : start + margin] = jnp.zeros(
                    ref.shape[:2] + (margin,) + ref.shape[3:], jnp.float32
                )

    edge = jnp.zeros((ks, comps, SUB, depth), jnp.float32)
    w_s[0] = edge
    w_s[groups + 1] = edge

    @pl.when(a == 0)
    def _():
        fwd_in[...] = jnp.zeros(fwd_in.shape, jnp.float32)

    pl.semaphore_wait(barrier, n_gy + n_gx - 2)

    def exchange(src, dst, send, recv, axis):
        size = n_gy if axis else n_gx
        copies = []
        for d in range(1, size):
            target = (a, lax.rem(b + d, n_gy)) if axis else (lax.rem(a + d, n_gx), b)
            copies.append(
                pltpu.make_async_remote_copy(
                    src_ref=src,
                    dst_ref=dst.at[d],
                    send_sem=send.at[d],
                    recv_sem=recv.at[d],
                    device_id=target,
                    device_id_type=MESH,
                )
            )
        for copy in copies:
            copy.start()
        return copies

    first = exchange(ag1.at[0], ag1, ag1_send, ag1_recv, 1)

    def halo(side):
        target = (a, b + 1) if side == 0 else (a, b - 1)
        start = inner - margin if side == 0 else 0
        place = 0 if side == 0 else margin + inner
        pairs = [(perf_s.at[0], perf_s.at[1 + side])]
        for src, dst in ((inv_h, inv_s), (rhs_h, rhs_s), (xc_h, xc_s), (yc_h, yc_s)):
            pairs.append(
                (src.at[:, :, pl.ds(start, margin)], dst.at[:, :, pl.ds(place, margin)])
            )
        return [
            pltpu.make_async_remote_copy(
                src_ref=src,
                dst_ref=dst,
                send_sem=halo_send.at[side, n],
                recv_sem=halo_recv.at[side, n],
                device_id=target,
                device_id_type=MESH,
            )
            for n, (src, dst) in enumerate(pairs)
        ]

    sends = ((0, b < n_gy - 1), (1, b > 0))
    receives = ((0, b > 0), (1, b < n_gy - 1))
    for side, present in sends:

        @pl.when(present)
        def _():
            for copy in halo(side):
                copy.start()

    for copy in first:
        copy.wait_recv()
    row = ag1[0]
    for d in range(1, n_gy):
        row = row + ag1[d]
    ag2[0] = row
    second = exchange(ag2.at[0], ag2, ag2_send, ag2_recv, 0)

    for copy in loads:
        copy.wait()
    for side, present in receives:

        @pl.when(present)
        def _():
            for copy in halo(side):
                copy.wait_recv()

    for copy in second:
        copy.wait_recv()
    wells = ag2[0]
    for d in range(1, n_gx):
        wells = wells + ag2[d]

    width = perf_s.shape[2]
    well_count = wells.shape[1]

    def perf_rows(slot):
        cell = perf_s[slot, 0:1].astype(jnp.int32)
        well = perf_s[slot, 1:2].astype(jnp.int32)
        line = lax.div(cell, depth)
        return line, cell - line * depth, well, perf_s[slot, 2:3]

    def well_hot(well):
        ids = lax.broadcasted_iota(jnp.int32, (well_count, width), 0)
        return (ids == well).astype(jnp.float32)

    def depth_hot(place):
        ids = lax.broadcasted_iota(jnp.int32, (depth, width), 0)
        return (ids == place).astype(jnp.float32)

    for slot, count, skip, start in (
        (0, inner, 0, margin),
        (1, margin, (inner - margin) * SUB, 0),
        (2, margin, 0, margin + inner),
    ):
        line, place, well, weight = perf_rows(slot)
        picked = jnp.dot(wells, well_hot(well), precision=HIGHEST)
        terms = picked * weight
        ids = lax.broadcasted_iota(jnp.int32, (count * SUB, width), 0) + skip
        hit = ids == line
        left = jnp.concatenate(
            [jnp.where(hit, terms[c : c + 1], 0.0) for c in range(comps)], axis=0
        )
        block = lax.dot_general(
            left, depth_hot(place), (((1,), (1,)), ((), ())), precision=HIGHEST
        )
        src_s[:, start : start + count] = block.reshape(comps, count, SUB, depth)

    sub = lax.broadcasted_iota(jnp.int32, (SUB, depth), 0)

    def load_inverse(g):
        return [[inv_s[c, d, g] for d in range(comps)] for c in range(comps)]

    def weigh(g, values):
        inverse = load_inverse(g)
        for k in range(ks):
            weighted = apply_inverse(inverse, values[k])
            for c in range(comps):
                v_s[g, k, c] = values[k][c]
                w_s[g + 1, k, c] = weighted[c]

    def solved(g):
        inverse = load_inverse(g)
        result = []
        for k in range(ks):
            rest = []
            for c in range(comps):
                here = w_s[g + 1, k, c]
                below = jnp.where(
                    sub == 0, pltpu.roll(w_s[g, k, c], 1, 0), pltpu.roll(here, 1, 0)
                )
                above = jnp.where(
                    sub == SUB - 1,
                    pltpu.roll(w_s[g + 2, k, c], SUB - 1, 0),
                    pltpu.roll(here, SUB - 1, 0),
                )
                rest.append(v_s[g, k, c] - yc_s[0, c, g] * below - yc_s[1, c, g] * above)
            result.append(apply_inverse(inverse, rest))
        return result

    def forward_copy(g):
        return pltpu.make_async_remote_copy(
            src_ref=q_s.at[g],
            dst_ref=fwd_in.at[g],
            send_sem=fwd_send.at[g],
            recv_sem=fwd_recv.at[g],
            device_id=(a + 1, b),
            device_id_type=MESH,
        )

    def turning_copy(g):
        return pltpu.make_async_remote_copy(
            src_ref=q_s.at[g],
            dst_ref=bwd_in.at[g],
            send_sem=bwd_send.at[g],
            recv_sem=bwd_recv.at[g],
            device_id=(a - 1, b),
            device_id_type=MESH,
        )

    def backward_copy(g):
        return pltpu.make_async_remote_copy(
            src_ref=p_s.at[g],
            dst_ref=bwd_in.at[g],
            send_sem=bwd_send.at[g],
            recv_sem=bwd_recv.at[g],
            device_id=(a - 1, b),
            device_id_type=MESH,
        )

    def forward_first(g):
        @pl.when(a > 0)
        def _():
            forward_copy(g).wait_recv()

        values = [
            [
                rhs_s[k, c, g] + src_s[c, g] - xc_s[0, c, g] * fwd_in[g, k, c]
                for c in range(comps)
            ]
            for k in range(ks)
        ]
        weigh(g, values)

    def forward_second(g):
        result = solved(g)
        for k in range(ks):
            for c in range(comps):
                q_s[g, k, c] = result[k][c]

        @pl.when(a < n_gx - 1)
        def _():
            forward_copy(g).start()

        if n_gx > 1:

            @pl.when(a == n_gx - 1)
            def _():
                turning_copy(g).start()

    def backward_first(g):
        backward_copy(g).wait_recv()
        values = [
            [xc_s[1, c, g] * bwd_in[g, k, c] for c in range(comps)] for k in range(ks)
        ]
        weigh(g, values)

    def backward_second(g):
        result = solved(g)
        for k in range(ks):
            for c in range(comps):
                p_s[g, k, c] = q_s[g, k, c] - result[k][c]

        @pl.when(a > 0)
        def _():
            backward_copy(g).start()

    def march(opening, closing):
        opening(0)

        def step(g, carry):
            opening(g)
            closing(g - 1)
            return carry

        lax.fori_loop(1, groups, step, 0)
        closing(groups - 1)

    march(forward_first, forward_second)

    @pl.when(a < n_gx - 1)
    def _():
        march(backward_first, backward_second)
        for k in range(ks):
            for c in range(comps):
                out_ref[k, c] = p_s[margin : margin + inner, k, c]

    @pl.when(a == n_gx - 1)
    def _():
        for k in range(ks):
            for c in range(comps):
                out_ref[k, c] = q_s[margin : margin + inner, k, c]

    line, place, well, weight = perf_rows(0)
    final = out_ref[ks - 1].reshape(comps * inner * SUB, depth)
    columns = jnp.dot(final, depth_hot(place), precision=HIGHEST)
    ids = lax.broadcasted_iota(jnp.int32, (inner * SUB, width), 0)
    hit = ids == line
    lines = inner * SUB
    sums = [
        jnp.sum(
            jnp.where(hit, columns[c * lines : (c + 1) * lines], 0.0), axis=0, keepdims=True
        )
        * weight
        for c in range(comps)
    ]
    sums.append(jnp.zeros((SUB - comps, width), jnp.float32))
    rs1[0] = lax.dot_general(
        jnp.concatenate(sums, axis=0),
        well_hot(well),
        (((1,), (1,)), ((), ())),
        precision=HIGHEST,
    )
    third = exchange(rs1.at[0], rs1, rs1_send, rs1_recv, 0)
    for copy in third:
        copy.wait_recv()
    column = rs1[0]
    for d in range(1, n_gx):
        column = column + rs1[d]
    rs2[0] = column
    fourth = exchange(rs2.at[0], rs2, rs2_send, rs2_recv, 1)

    for copy in first + second + third:
        copy.wait_send()
    for side, present in sends:

        @pl.when(present)
        def _():
            for copy in halo(side):
                copy.wait_send()

    def drain(make):
        def step(g, carry):
            make(g).wait_send()
            return carry

        lax.fori_loop(0, groups, step, 0)

    @pl.when(a < n_gx - 1)
    def _():
        drain(forward_copy)

    @pl.when(a > 0)
    def _():
        drain(backward_copy)

    for copy in fourth:
        copy.wait()
    total = rs2[0]
    for d in range(1, n_gy):
        total = total + rs2[d]
    total = total[0:comps]
    picked = [
        jnp.sum(jnp.where(lane == first_well + w, total, 0.0), axis=1, keepdims=True)
        for w in range(own_wells)
    ]
    update_ref[...] = jnp.concatenate(picked, axis=1)


def per_device(
    n_gx,
    n_gy,
    adjoint_rhs,
    block_inverse,
    x_couplings,
    y_couplings,
    perf_cell,
    perf_well,
    perf_weight,
    well_adjoint,
):
    ks, comps, planes, lines, depth = adjoint_rhs.shape
    assert planes == 1 and lines % SUB == 0
    inner = lines // SUB
    margin = round_up(2 * n_gx - 1, SUB) // SUB
    assert margin <= inner
    groups = inner + 2 * margin
    perfs = perf_cell.shape[0]
    own_wells = well_adjoint.shape[1]
    well_lanes = round_up(own_wells * n_gx * n_gy, LANES)
    perf_lanes = round_up(perfs, LANES)
    dims = (n_gx, n_gy, ks, comps, inner, margin, depth, perfs, own_wells)

    def grouped(array):
        return array.reshape(array.shape[:2] + (inner, SUB, depth))

    vmem = pl.BlockSpec(memory_space=pltpu.VMEM)
    hbm = pl.BlockSpec(memory_space=pl.ANY)
    f32 = jnp.float32
    dma = pltpu.SemaphoreType.DMA
    wide = lambda d0, d1: pltpu.VMEM((d0, d1, groups, SUB, depth), f32)
    flow = lambda extra: pltpu.VMEM((groups + extra, ks, comps, SUB, depth), f32)
    tiles = lambda count: pltpu.VMEM((count, SUB, well_lanes), f32)
    precond, update = pl.pallas_call(
        functools.partial(kernel, dims),
        out_shape=(
            jax.ShapeDtypeStruct((ks, comps, inner, SUB, depth), f32),
            jax.ShapeDtypeStruct((comps, own_wells), f32),
        ),
        in_specs=[hbm] * 4 + [vmem] * 4,
        out_specs=(vmem, vmem),
        scratch_shapes=[
            wide(ks, comps),
            wide(comps, comps),
            wide(2, comps),
            wide(2, comps),
            pltpu.VMEM((comps, groups, SUB, depth), f32),
            flow(0),
            flow(0),
            flow(0),
            flow(0),
            flow(0),
            flow(2),
            pltpu.VMEM((3, SUB, perf_lanes), f32),
            tiles(n_gy),
            tiles(n_gx),
            tiles(n_gx),
            tiles(n_gy),
            dma((4,)),
            dma((2, 5)),
            dma((2, 5)),
            dma((n_gy,)),
            dma((n_gy,)),
            dma((n_gx,)),
            dma((n_gx,)),
            dma((n_gx,)),
            dma((n_gx,)),
            dma((n_gy,)),
            dma((n_gy,)),
            dma((groups,)),
            dma((groups,)),
            dma((groups,)),
            dma((groups,)),
        ],
        compiler_params=pltpu.CompilerParams(collective_id=0, has_side_effects=True),
    )(
        grouped(adjoint_rhs),
        grouped(block_inverse),
        grouped(x_couplings),
        grouped(y_couplings),
        perf_cell.reshape(1, perfs),
        perf_well.reshape(1, perfs),
        perf_weight.reshape(1, perfs),
        well_adjoint,
    )
    return precond.reshape(adjoint_rhs.shape), update


def solution(mesh):
    placed = (
        P(None, None, "gx", "gy", None),
        P(None, None, "gx", "gy", None),
        P(None, None, "gx", "gy", None),
        P(None, None, "gx", "gy", None),
        P(("gx", "gy")),
        P(("gx", "gy")),
        P(("gx", "gy")),
        P(None, ("gx", "gy")),
    )
    return jax.shard_map(
        functools.partial(per_device, mesh.shape["gx"], mesh.shape["gy"]),
        mesh=mesh,
        in_specs=placed,
        out_specs=(P(None, None, "gx", "gy", None), P(None, ("gx", "gy"))),
        check_vma=False,
    )
```

time: 185 us -> 45.4 us (0.25)
  the two profiles are of different devices: /device:TPU:0 before, /device:TPU:9 now
where the time goes in v1:
time: 45.4 us; the launch traced here: 45.3 us
  Pallas kernels  42.4 us (93%)
  local copies, waits for them, and re-layouts  2.2 us (5%)
  between operations  0.65 us (1%)
    pallas_call x1, Pallas kernels, per_device(): pl.pallas_call(functools.partial(kernel, dims), out_shape=(jax.ShapeDtype...  42.4 us
    unnamed x4, local copies, waits for them, and re-layouts  2.2 us

profile of v1, /device:TPU:9, one launch (start us, length us, event | category | flops | bytes accessed | tf_op | source)
XLA Modules:
  0.0 45.3 jit_solution(3476003125071713869)
XLA Ops:
  0.6 42.4 %shard_map.95 = (f32[2,3,8,8,128]{4,3,2,1,0:T(8,128)}, f32[3,4]{1,0:T(4,128)}) custom-call(f32[2,3,8,8,128]{4,3,2,1,0:T(8,128)} %bitcast.12, f32[3,3,8,8,128]{4,3,2,1,0:T(8,128)} %bitcast.10, f32[2,3,8,8,128]{4,3,2,1,0:T(8,128)} %bitcast.13, f32[2,3,8,8,128]{4,3,2,1,0:T(8,128)} %bitcast.14, s32[1,64]{1,0:T(1,128)} %bitcast.15, s32[1,64]{1,0:T(1,128)} %bitcast.16, ...), custom_call_target="tpu_custom_call" | custom-call | tf_op jit(solution)/shard_map/pallas_call | solution.py:476
  43.0 0.0 copy-start
  43.1 1.6 %copy.13 = f32[2,3,1,64,128]{4,3,2,1,0:T(8,128)} copy(f32[2,3,1,64,128]{4,3,2,1,0:T(8,128)} %bitcast.11) | data formatting | bytes 393216
  44.7 0.0 copy-done
  44.7 0.6 %copy.14 = f32[3,4]{1,0:T(4,128)} copy(f32[3,4]{1,0:T(4,128)S(1)} %copy-done) | data formatting | bytes 96
Async XLA Ops:
  43.0 1.6 %copy-start = (f32[3,4]{1,0:T(4,128)S(1)}, f32[3,4]{1,0:T(4,128)}, u32[]{:S(2)}) copy-start(f32[3,4]{1,0:T(4,128)} %get-tuple-element.11) | copy-start | bytes 148

commit v2 on v1

--- a/solution.py
+++ b/solution.py
@@ -56,6 +56,8 @@
     ag2,
     rs1,
     rs2,
+    well_hot,
+    depth_hot,
     load_sem,
     halo_send,
     halo_recv,
@@ -120,8 +122,8 @@
                 )
 
     edge = jnp.zeros((ks, comps, SUB, depth), jnp.float32)
-    w_s[0] = edge
-    w_s[groups + 1] = edge
+    w_s[:, 0] = edge
+    w_s[:, groups + 1] = edge
 
     @pl.when(a == 0)
     def _():
@@ -129,7 +131,7 @@
 
     pl.semaphore_wait(barrier, n_gy + n_gx - 2)
 
-    def exchange(src, dst, send, recv, axis):
+    def exchanged(src, dst, send, recv, axis):
         size = n_gy if axis else n_gx
         copies = []
         for d in range(1, size):
@@ -144,6 +146,10 @@
                     device_id_type=MESH,
                 )
             )
+        return copies
+
+    def exchange(*args):
+        copies = exchanged(*args)
         for copy in copies:
             copy.start()
         return copies
@@ -180,6 +186,24 @@
             for copy in halo(side):
                 copy.start()
 
+    width = perf_s.shape[2]
+    well_count = ag1.shape[2]
+
+    def perf_rows(slot):
+        cell = perf_s[slot, 0:1].astype(jnp.int32)
+        well = perf_s[slot, 1:2].astype(jnp.int32)
+        line = lax.div(cell, depth)
+        return line, cell - line * depth, well, perf_s[slot, 2:3]
+
+    def make_hot(slot):
+        _, place, well, _ = perf_rows(slot)
+        ids = lax.broadcasted_iota(jnp.int32, (well_count, width), 0)
+        well_hot[slot] = (ids == well).astype(jnp.float32)
+        ids = lax.broadcasted_iota(jnp.int32, (depth, width), 0)
+        depth_hot[slot] = (ids == place).astype(jnp.float32)
+
+    make_hot(0)
+
     for copy in first:
         copy.wait_recv()
     row = ag1[0]
@@ -197,36 +221,21 @@
             for copy in halo(side):
                 copy.wait_recv()
 
+    make_hot(1)
+    make_hot(2)
     for copy in second:
         copy.wait_recv()
     wells = ag2[0]
     for d in range(1, n_gx):
         wells = wells + ag2[d]
 
-    width = perf_s.shape[2]
-    well_count = wells.shape[1]
-
-    def perf_rows(slot):
-        cell = perf_s[slot, 0:1].astype(jnp.int32)
-        well = perf_s[slot, 1:2].astype(jnp.int32)
-        line = lax.div(cell, depth)
-        return line, cell - line * depth, well, perf_s[slot, 2:3]
-
-    def well_hot(well):
-        ids = lax.broadcasted_iota(jnp.int32, (well_count, width), 0)
-        return (ids == well).astype(jnp.float32)
-
-    def depth_hot(place):
-        ids = lax.broadcasted_iota(jnp.int32, (depth, width), 0)
-        return (ids == place).astype(jnp.float32)
-
     for slot, count, skip, start in (
         (0, inner, 0, margin),
         (1, margin, (inner - margin) * SUB, 0),
         (2, margin, 0, margin + inner),
     ):
-        line, place, well, weight = perf_rows(slot)
-        picked = jnp.dot(wells, well_hot(well), precision=HIGHEST)
+        line, _, _, weight = perf_rows(slot)
+        picked = jnp.dot(wells, well_hot[slot], precision=HIGHEST)
         terms = picked * weight
         ids = lax.broadcasted_iota(jnp.int32, (count * SUB, width), 0) + skip
         hit = ids == line
@@ -234,7 +243,7 @@
             [jnp.where(hit, terms[c : c + 1], 0.0) for c in range(comps)], axis=0
         )
         block = lax.dot_general(
-            left, depth_hot(place), (((1,), (1,)), ((), ())), precision=HIGHEST
+            left, depth_hot[slot], (((1,), (1,)), ((), ())), precision=HIGHEST
         )
         src_s[:, start : start + count] = block.reshape(comps, count, SUB, depth)
 
@@ -243,157 +252,157 @@
     def load_inverse(g):
         return [[inv_s[c, d, g] for d in range(comps)] for c in range(comps)]
 
-    def weigh(g, values):
-        inverse = load_inverse(g)
-        for k in range(ks):
-            weighted = apply_inverse(inverse, values[k])
-            for c in range(comps):
-                v_s[g, k, c] = values[k][c]
-                w_s[g + 1, k, c] = weighted[c]
-
-    def solved(g):
-        inverse = load_inverse(g)
-        result = []
-        for k in range(ks):
-            rest = []
-            for c in range(comps):
-                here = w_s[g + 1, k, c]
-                below = jnp.where(
-                    sub == 0, pltpu.roll(w_s[g, k, c], 1, 0), pltpu.roll(here, 1, 0)
-                )
-                above = jnp.where(
-                    sub == SUB - 1,
-                    pltpu.roll(w_s[g + 2, k, c], SUB - 1, 0),
-                    pltpu.roll(here, SUB - 1, 0),
-                )
-                rest.append(v_s[g, k, c] - yc_s[0, c, g] * below - yc_s[1, c, g] * above)
-            result.append(apply_inverse(inverse, rest))
-        return result
-
-    def forward_copy(g):
+    def weigh(k, g, values):
+        weighted = apply_inverse(load_inverse(g), values)
+        for c in range(comps):
+            v_s[k, g, c] = values[c]
+            w_s[k, g + 1, c] = weighted[c]
+
+    def solved(k, g):
+        rest = []
+        for c in range(comps):
+            here = w_s[k, g + 1, c]
+            below = jnp.where(
+                sub == 0, pltpu.roll(w_s[k, g, c], 1, 0), pltpu.roll(here, 1, 0)
+            )
+            above = jnp.where(
+                sub == SUB - 1,
+                pltpu.roll(w_s[k, g + 2, c], SUB - 1, 0),
+                pltpu.roll(here, SUB - 1, 0),
+            )
+            rest.append(v_s[k, g, c] - yc_s[0, c, g] * below - yc_s[1, c, g] * above)
+        return apply_inverse(load_inverse(g), rest)
+
+    def forward_copy(k, g):
         return pltpu.make_async_remote_copy(
-            src_ref=q_s.at[g],
-            dst_ref=fwd_in.at[g],
-            send_sem=fwd_send.at[g],
-            recv_sem=fwd_recv.at[g],
+            src_ref=q_s.at[k, g],
+            dst_ref=fwd_in.at[k, g],
+            send_sem=fwd_send.at[k, g],
+            recv_sem=fwd_recv.at[k, g],
             device_id=(a + 1, b),
             device_id_type=MESH,
         )
 
-    def turning_copy(g):
+    def backward_copy(k, g, src):
         return pltpu.make_async_remote_copy(
-            src_ref=q_s.at[g],
-            dst_ref=bwd_in.at[g],
-            send_sem=bwd_send.at[g],
-            recv_sem=bwd_recv.at[g],
+            src_ref=src.at[k, g],
+            dst_ref=bwd_in.at[k, g],
+            send_sem=bwd_send.at[k, g],
+            recv_sem=bwd_recv.at[k, g],
             device_id=(a - 1, b),
             device_id_type=MESH,
         )
 
-    def backward_copy(g):
-        return pltpu.make_async_remote_copy(
-            src_ref=p_s.at[g],
-            dst_ref=bwd_in.at[g],
-            send_sem=bwd_send.at[g],
-            recv_sem=bwd_recv.at[g],
-            device_id=(a - 1, b),
-            device_id_type=MESH,
-        )
-
-    def forward_first(g):
+    def forward_first(k, g):
         @pl.when(a > 0)
         def _():
-            forward_copy(g).wait_recv()
-
-        values = [
+            forward_copy(k, g).wait_recv()
+
+        weigh(
+            k,
+            g,
             [
-                rhs_s[k, c, g] + src_s[c, g] - xc_s[0, c, g] * fwd_in[g, k, c]
+                rhs_s[k, c, g] + src_s[c, g] - xc_s[0, c, g] * fwd_in[k, g, c]
                 for c in range(comps)
-            ]
-            for k in range(ks)
+            ],
+        )
+
+    def forward_second(k, g):
+        result = solved(k, g)
+        for c in range(comps):
+            q_s[k, g, c] = result[c]
+
+        @pl.when(a < n_gx - 1)
+        def _():
+            forward_copy(k, g).start()
+
+        @pl.when(a == n_gx - 1)
+        def _():
+            backward_copy(k, g, q_s).start()
+
+    def backward_first(k, g):
+        backward_copy(k, g, p_s).wait_recv()
+        weigh(k, g, [xc_s[1, c, g] * bwd_in[k, g, c] for c in range(comps)])
+
+    def backward_second(k, g):
+        result = solved(k, g)
+        for c in range(comps):
+            p_s[k, g, c] = q_s[k, g, c] - result[c]
+
+        @pl.when(a > 0)
+        def _():
+            backward_copy(k, g, p_s).start()
+
+    def march(k, opening, closing):
+        opening(k, 0)
+
+        def step(g, carry):
+            opening(k, g)
+            closing(k, g - 1)
+            return carry
+
+        lax.fori_loop(1, groups, step, 0)
+        closing(k, groups - 1)
+
+    def deliver(k, source):
+        for c in range(comps):
+            out_ref[k, c] = source[k, margin : margin + inner, c]
+
+    def well_sums():
+        line, _, _, weight = perf_rows(0)
+        lines = inner * SUB
+        final = out_ref[ks - 1].reshape(comps * lines, depth)
+        columns = jnp.dot(final, depth_hot[0], precision=HIGHEST)
+        ids = lax.broadcasted_iota(jnp.int32, (lines, width), 0)
+        hit = ids == line
+        sums = [
+            jnp.sum(
+                jnp.where(hit, columns[c * lines : (c + 1) * lines], 0.0),
+                axis=0,
+                keepdims=True,
+            )
+            * weight
+            for c in range(comps)
         ]
-        weigh(g, values)
-
-    def forward_second(g):
-        result = solved(g)
-        for k in range(ks):
-            for c in range(comps):
-                q_s[g, k, c] = result[k][c]
-
-        @pl.when(a < n_gx - 1)
-        def _():
-            forward_copy(g).start()
-
-        if n_gx > 1:
-
-            @pl.when(a == n_gx - 1)
-            def _():
-                turning_copy(g).start()
-
-    def backward_first(g):
-        backward_copy(g).wait_recv()
-        values = [
-            [xc_s[1, c, g] * bwd_in[g, k, c] for c in range(comps)] for k in range(ks)
-        ]
-        weigh(g, values)
-
-    def backward_second(g):
-        result = solved(g)
-        for k in range(ks):
-            for c in range(comps):
-                p_s[g, k, c] = q_s[g, k, c] - result[k][c]
-
-        @pl.when(a > 0)
-        def _():
-            backward_copy(g).start()
-
-    def march(opening, closing):
-        opening(0)
-
-        def step(g, carry):
-            opening(g)
-            closing(g - 1)
-            return carry
-
-        lax.fori_loop(1, groups, step, 0)
-        closing(groups - 1)
-
-    march(forward_first, forward_second)
+        sums.append(jnp.zeros((SUB - comps, width), jnp.float32))
+        rs1[0] = lax.dot_general(
+            jnp.concatenate(sums, axis=0),
+            well_hot[0],
+            (((1,), (1,)), ((), ())),
+            precision=HIGHEST,
+        )
+        for copy in exchanged(rs1.at[0], rs1, rs1_send, rs1_recv, 0):
+            copy.start()
+
+    order = range(ks - 1, -1, -1)
+    for k in order:
+        march(k, forward_first, forward_second)
+
+    @pl.when(a == n_gx - 1)
+    def _():
+        for k in order:
+            deliver(k, q_s)
 
     @pl.when(a < n_gx - 1)
     def _():
-        march(backward_first, backward_second)
-        for k in range(ks):
-            for c in range(comps):
-                out_ref[k, c] = p_s[margin : margin + inner, k, c]
-
-    @pl.when(a == n_gx - 1)
-    def _():
-        for k in range(ks):
-            for c in range(comps):
-                out_ref[k, c] = q_s[margin : margin + inner, k, c]
-
-    line, place, well, weight = perf_rows(0)
-    final = out_ref[ks - 1].reshape(comps * inner * SUB, depth)
-    columns = jnp.dot(final, depth_hot(place), precision=HIGHEST)
-    ids = lax.broadcasted_iota(jnp.int32, (inner * SUB, width), 0)
-    hit = ids == line
-    lines = inner * SUB
-    sums = [
-        jnp.sum(
-            jnp.where(hit, columns[c * lines : (c + 1) * lines], 0.0), axis=0, keepdims=True
-        )
-        * weight
-        for c in range(comps)
-    ]
-    sums.append(jnp.zeros((SUB - comps, width), jnp.float32))
-    rs1[0] = lax.dot_general(
-        jnp.concatenate(sums, axis=0),
-        well_hot(well),
-        (((1,), (1,)), ((), ())),
-        precision=HIGHEST,
-    )
-    third = exchange(rs1.at[0], rs1, rs1_send, rs1_recv, 0)
+        march(ks - 1, backward_first, backward_second)
+        deliver(ks - 1, p_s)
+
+    @pl.when(a == 0)
+    def _():
+        well_sums()
+
+    @pl.when(a < n_gx - 1)
+    def _():
+        for k in order[1:]:
+            march(k, backward_first, backward_second)
+            deliver(k, p_s)
+
+    @pl.when(a > 0)
+    def _():
+        well_sums()
+
+    third = exchanged(rs1.at[0], rs1, rs1_send, rs1_recv, 0)
     for copy in third:
         copy.wait_recv()
     column = rs1[0]
@@ -412,11 +421,13 @@
                 copy.wait_send()
 
     def drain(make):
-        def step(g, carry):
-            make(g).wait_send()
-            return carry
-
-        lax.fori_loop(0, groups, step, 0)
+        for k in range(ks):
+
+            def step(g, carry):
+                make(k, g).wait_send()
+                return carry
+
+            lax.fori_loop(0, groups, step, 0)
 
     @pl.when(a < n_gx - 1)
     def _():
@@ -424,7 +435,7 @@
 
     @pl.when(a > 0)
     def _():
-        drain(backward_copy)
+        drain(lambda k, g: backward_copy(k, g, p_s))
 
     for copy in fourth:
         copy.wait()
@@ -452,7 +463,7 @@
     well_adjoint,
 ):
     ks, comps, planes, lines, depth = adjoint_rhs.shape
-    assert planes == 1 and lines % SUB == 0
+    assert planes == 1 and n_gx > 1 and lines % SUB == 0
     inner = lines // SUB
     margin = round_up(2 * n_gx - 1, SUB) // SUB
     assert margin <= inner
@@ -471,13 +482,13 @@
     f32 = jnp.float32
     dma = pltpu.SemaphoreType.DMA
     wide = lambda d0, d1: pltpu.VMEM((d0, d1, groups, SUB, depth), f32)
-    flow = lambda extra: pltpu.VMEM((groups + extra, ks, comps, SUB, depth), f32)
+    flow = lambda extra: pltpu.VMEM((ks, groups + extra, comps, SUB, depth), f32)
     tiles = lambda count: pltpu.VMEM((count, SUB, well_lanes), f32)
     precond, update = pl.pallas_call(
         functools.partial(kernel, dims),
         out_shape=(
-            jax.ShapeDtypeStruct((ks, comps, inner, SUB, depth), f32),
-            jax.ShapeDtypeStruct((comps, own_wells), f32),
+            pltpu.VMEM((ks, comps, inner, SUB, depth), f32),
+            pltpu.VMEM((comps, own_wells), f32),
         ),
         in_specs=[hbm] * 4 + [vmem] * 4,
         out_specs=(vmem, vmem),
@@ -498,6 +509,8 @@
             tiles(n_gx),
             tiles(n_gx),
             tiles(n_gy),
+            pltpu.VMEM((3, well_lanes, perf_lanes), f32),
+            pltpu.VMEM((3, depth, perf_lanes), f32),
             dma((4,)),
             dma((2, 5)),
             dma((2, 5)),
@@ -509,10 +522,10 @@
             dma((n_gx,)),
             dma((n_gy,)),
             dma((n_gy,)),
-            dma((groups,)),
-            dma((groups,)),
-            dma((groups,)),
-            dma((groups,)),
+            dma((ks, groups)),
+            dma((ks, groups)),
+            dma((ks, groups)),
+            dma((ks, groups)),
         ],
         compiler_params=pltpu.CompilerParams(collective_id=0, has_side_effects=True),
     )(

time: 45.4 us -> 41.8 us (0.921)
  the two profiles are of different devices: /device:TPU:9 before, /device:TPU:0 now
where the time goes in v2:
time: 41.8 us; the launch traced here: 41.6 us
  Pallas kernels  39.7 us (95%)
  local copies, waits for them, and re-layouts  1.26 us (3%)
  between operations  0.64 us (2%)
    pallas_call x1, Pallas kernels, per_device(): pl.pallas_call(functools.partial(kernel, dims), out_shape=(pltpu.VMEM((ks...  39.7 us
    unnamed x2, local copies, waits for them, and re-layouts  1.26 us

profile of v2, /device:TPU:0, one launch (start us, length us, event | category | flops | bytes accessed | tf_op | source)
XLA Modules:
  0.0 41.6 jit_solution(6428028861290942980)
XLA Ops:
  0.6 39.7 %shard_map.95 = (f32[2,3,8,8,128]{4,3,2,1,0:T(8,128)S(1)}, f32[3,4]{1,0:T(4,128)S(1)}) custom-call(f32[2,3,8,8,128]{4,3,2,1,0:T(8,128)} %bitcast.12, f32[3,3,8,8,128]{4,3,2,1,0:T(8,128)} %bitcast.11, f32[2,3,8,8,128]{4,3,2,1,0:T(8,128)} %bitcast.13, f32[2,3,8,8,128]{4,3,2,1,0:T(8,128)} %bitcast.14, s32[1,64]{1,0:T(1,128)} %bitcast.15, s32[1,64]{1,0:T(1,128)} %bitcast.16, ...), custom_call_target="tpu_custom_call" | custom-call | tf_op jit(solution)/shard_map/pallas_call | solution.py:487
  40.3 0.7 %copy.13 = f32[2,3,1,64,128]{4,3,2,1,0:T(8,128)} copy(f32[2,3,1,64,128]{4,3,2,1,0:T(8,128)S(1)} %bitcast.10) | data formatting | bytes 393216
  41.0 0.6 %copy.14 = f32[3,4]{1,0:T(4,128)} copy(f32[3,4]{1,0:T(4,128)S(1)} %get-tuple-element.9) | data formatting | bytes 96

commit v3 on v2

--- a/solution.py
+++ b/solution.py
@@ -10,11 +10,23 @@
 MESH = pl.DeviceIdType.MESH
 SUB = 8
 LANES = 128
-HIGHEST = lax.Precision.HIGHEST
 
 
 def round_up(value, step):
     return -(-value // step) * step
+
+
+def dot_exact(values, hot, contract):
+    rows = values.shape[0]
+    high = values.astype(jnp.bfloat16)
+    rest = values - high.astype(jnp.float32)
+    middle = rest.astype(jnp.bfloat16)
+    low = (rest - middle.astype(jnp.float32)).astype(jnp.bfloat16)
+    dims = (((1,), (contract,)), ((), ()))
+    return sum(
+        lax.dot_general(part, hot, dims, preferred_element_type=jnp.float32)
+        for part in (low, middle, high)
+    )
 
 
 def apply_inverse(inverse, values):
@@ -198,9 +210,9 @@
     def make_hot(slot):
         _, place, well, _ = perf_rows(slot)
         ids = lax.broadcasted_iota(jnp.int32, (well_count, width), 0)
-        well_hot[slot] = (ids == well).astype(jnp.float32)
+        well_hot[slot] = (ids == well).astype(jnp.float32).astype(jnp.bfloat16)
         ids = lax.broadcasted_iota(jnp.int32, (depth, width), 0)
-        depth_hot[slot] = (ids == place).astype(jnp.float32)
+        depth_hot[slot] = (ids == place).astype(jnp.float32).astype(jnp.bfloat16)
 
     make_hot(0)
 
@@ -235,16 +247,14 @@
         (2, margin, 0, margin + inner),
     ):
         line, _, _, weight = perf_rows(slot)
-        picked = jnp.dot(wells, well_hot[slot], precision=HIGHEST)
+        picked = dot_exact(wells, well_hot[slot], 0)
         terms = picked * weight
         ids = lax.broadcasted_iota(jnp.int32, (count * SUB, width), 0) + skip
         hit = ids == line
         left = jnp.concatenate(
             [jnp.where(hit, terms[c : c + 1], 0.0) for c in range(comps)], axis=0
         )
-        block = lax.dot_general(
-            left, depth_hot[slot], (((1,), (1,)), ((), ())), precision=HIGHEST
-        )
+        block = dot_exact(left, depth_hot[slot], 1)
         src_s[:, start : start + count] = block.reshape(comps, count, SUB, depth)
 
     sub = lax.broadcasted_iota(jnp.int32, (SUB, depth), 0)
@@ -352,7 +362,7 @@
         line, _, _, weight = perf_rows(0)
         lines = inner * SUB
         final = out_ref[ks - 1].reshape(comps * lines, depth)
-        columns = jnp.dot(final, depth_hot[0], precision=HIGHEST)
+        columns = dot_exact(final, depth_hot[0], 0)
         ids = lax.broadcasted_iota(jnp.int32, (lines, width), 0)
         hit = ids == line
         sums = [
@@ -365,12 +375,7 @@
             for c in range(comps)
         ]
         sums.append(jnp.zeros((SUB - comps, width), jnp.float32))
-        rs1[0] = lax.dot_general(
-            jnp.concatenate(sums, axis=0),
-            well_hot[0],
-            (((1,), (1,)), ((), ())),
-            precision=HIGHEST,
-        )
+        rs1[0] = dot_exact(jnp.concatenate(sums, axis=0), well_hot[0], 1)
         for copy in exchanged(rs1.at[0], rs1, rs1_send, rs1_recv, 0):
             copy.start()
 
@@ -509,8 +514,8 @@
             tiles(n_gx),
             tiles(n_gx),
             tiles(n_gy),
-            pltpu.VMEM((3, well_lanes, perf_lanes), f32),
-            pltpu.VMEM((3, depth, perf_lanes), f32),
+            pltpu.VMEM((3, well_lanes, perf_lanes), jnp.bfloat16),
+            pltpu.VMEM((3, depth, perf_lanes), jnp.bfloat16),
             dma((4,)),
             dma((2, 5)),
             dma((2, 5)),

time: 41.8 us -> 41.1 us (0.983)
  Pallas kernels: 39.7 us -> 39 us
    pallas_call x1, Pallas kernels: 39.7 us -> 39 us  [per_device(): pl.pallas_call(functools.partial(kernel, dims), out_shape=(pltpu.VMEM((ks...]
where the time goes in v3:
time: 41.1 us; the launch traced here: 40.9 us
  Pallas kernels  39 us (95%)
  local copies, waits for them, and re-layouts  1.26 us (3%)
  between operations  0.64 us (2%)
    pallas_call x1, Pallas kernels, per_device(): pl.pallas_call(functools.partial(kernel, dims), out_shape=(pltpu.VMEM((ks...  39 us
    unnamed x2, local copies, waits for them, and re-layouts  1.26 us

profile of v3, /device:TPU:0, one launch (start us, length us, event | category | flops | bytes accessed | tf_op | source)
XLA Modules:
  0.0 40.9 jit_solution(6990879921719581814)
XLA Ops:
  0.6 39.0 %shard_map.95 = (f32[2,3,8,8,128]{4,3,2,1,0:T(8,128)S(1)}, f32[3,4]{1,0:T(4,128)S(1)}) custom-call(f32[2,3,8,8,128]{4,3,2,1,0:T(8,128)} %bitcast.12, f32[3,3,8,8,128]{4,3,2,1,0:T(8,128)} %bitcast.11, f32[2,3,8,8,128]{4,3,2,1,0:T(8,128)} %bitcast.13, f32[2,3,8,8,128]{4,3,2,1,0:T(8,128)} %bitcast.14, s32[1,64]{1,0:T(1,128)} %bitcast.15, s32[1,64]{1,0:T(1,128)} %bitcast.16, ...), custom_call_target="tpu_custom_call" | custom-call | tf_op jit(solution)/shard_map/pallas_call | solution.py:492
  39.7 0.7 %copy.13 = f32[2,3,1,64,128]{4,3,2,1,0:T(8,128)} copy(f32[2,3,1,64,128]{4,3,2,1,0:T(8,128)S(1)} %bitcast.10) | data formatting | bytes 393216
  40.3 0.6 %copy.14 = f32[3,4]{1,0:T(4,128)} copy(f32[3,4]{1,0:T(4,128)S(1)} %get-tuple-element.9) | data formatting | bytes 96

commit v4 on v3

--- a/solution.py
+++ b/solution.py
@@ -191,12 +191,15 @@
 
     sends = ((0, b < n_gy - 1), (1, b > 0))
     receives = ((0, b > 0), (1, b < n_gy - 1))
-    for side, present in sends:
-
-        @pl.when(present)
-        def _():
-            for copy in halo(side):
-                copy.start()
+    def send_halo(chosen):
+        for side, present in sends:
+
+            @pl.when(chosen & present)
+            def _():
+                for copy in halo(side):
+                    copy.start()
+
+    send_halo(a == 0)
 
     width = perf_s.shape[2]
     well_count = ag1.shape[2]
@@ -223,6 +226,7 @@
         row = row + ag1[d]
     ag2[0] = row
     second = exchange(ag2.at[0], ag2, ag2_send, ag2_recv, 0)
+    send_halo(a > 0)
 
     for copy in loads:
         copy.wait()
@@ -393,7 +397,7 @@
         march(ks - 1, backward_first, backward_second)
         deliver(ks - 1, p_s)
 
-    @pl.when(a == 0)
+    @pl.when(a < n_gx - 1)
     def _():
         well_sums()
 
@@ -403,7 +407,7 @@
             march(k, backward_first, backward_second)
             deliver(k, p_s)
 
-    @pl.when(a > 0)
+    @pl.when(a == n_gx - 1)
     def _():
         well_sums()
 

time: 41.1 us -> 41 us (level)
  no operation moved by 1% of the time
where the time goes in v4:
time: 41 us; the launch traced here: 40.8 us
  Pallas kernels  38.9 us (95%)
  local copies, waits for them, and re-layouts  1.26 us (3%)
  between operations  0.64 us (2%)
    pallas_call x1, Pallas kernels, per_device(): pl.pallas_call(functools.partial(kernel, dims), out_shape=(pltpu.VMEM((ks...  38.9 us
    unnamed x2, local copies, waits for them, and re-layouts  1.26 us

profile of v4, /device:TPU:0, one launch (start us, length us, event | category | flops | bytes accessed | tf_op | source)
XLA Modules:
  0.0 40.8 jit_solution(6884414239595732636)
XLA Ops:
  0.6 38.9 %shard_map.95 = (f32[2,3,8,8,128]{4,3,2,1,0:T(8,128)S(1)}, f32[3,4]{1,0:T(4,128)S(1)}) custom-call(f32[2,3,8,8,128]{4,3,2,1,0:T(8,128)} %bitcast.12, f32[3,3,8,8,128]{4,3,2,1,0:T(8,128)} %bitcast.11, f32[2,3,8,8,128]{4,3,2,1,0:T(8,128)} %bitcast.13, f32[2,3,8,8,128]{4,3,2,1,0:T(8,128)} %bitcast.14, s32[1,64]{1,0:T(1,128)} %bitcast.15, s32[1,64]{1,0:T(1,128)} %bitcast.16, ...), custom_call_target="tpu_custom_call" | custom-call | tf_op jit(solution)/shard_map/pallas_call | solution.py:496
  39.6 0.7 %copy.13 = f32[2,3,1,64,128]{4,3,2,1,0:T(8,128)} copy(f32[2,3,1,64,128]{4,3,2,1,0:T(8,128)S(1)} %bitcast.10) | data formatting | bytes 393216
  40.3 0.6 %copy.14 = f32[3,4]{1,0:T(4,128)} copy(f32[3,4]{1,0:T(4,128)S(1)} %get-tuple-element.9) | data formatting | bytes 96
